TPU v7x, 128 devices: a whole 4x4x4 slice. The times are simulated.
128 devices in a mesh: ctx: 8 (over z, y_hi), tp: 16 (over y_lo, x, core).
Axes of the slice: x: 4, y: 4 (y_hi: 2, y_lo: 2; y = y_hi * 2 + y_lo), z: 4, core: 2. Of those that a mesh axis runs over, the one named last changes fastest.
Arguments:
- byte_embeds: bfloat16 [24576, 1024], P(('ctx', 'tp')), may hold values from -6 to 6
- local_embeds: bfloat16 [24576, 1024], P(('ctx', 'tp')), may hold values from -6 to 6
- global_qkv: bfloat16 [3, 8192, 4096], P(None, None, 'tp'), may hold values from -0.0625 to 0.0625
- global_out: bfloat16 [4096, 8192], P('tp'), may hold values from -1.5 to 1.5
- local_qkv: bfloat16 [1, 1024, 3072], replicated, may hold values from -0.1875 to 0.1875
- local_out: bfloat16 [1, 1024, 1024], replicated, may hold values from -0.1875 to 0.1875
- cotangent: bfloat16 [24576, 1024], P(('ctx', 'tp')), may hold values from -6 to 6
Outputs:
- hidden: bfloat16 [24576, 1024], P(('ctx', 'tp'))
- grad_qkv: float32 [1, 1024, 3072], P(None, ('ctx', 'tp'))
- grad_out: float32 [1, 1024, 1024], P(None, ('ctx', 'tp'))
All inputs are finite; a program needn't handle non-finite values.
Results may differ from a plain program's by a relative error of at most 0.028.
Values may be sent and summed in bfloat16 or wider, within the bound.
A program may use at most 128 MiB of HBM per device.

v0:
```python
import math
import jax
import jax.numpy as jnp
from jax import lax
from jax.sharding import PartitionSpec as P

PATCH = 8
HEAD_DIM = 128
LOCAL_HEADS = 8
LOCAL_HEAD_DIM = 128


def from_behind(value, axis, steps):
    count = lax.axis_size(axis)
    initial, last = (max(0, -steps), min(count, count - steps))
    return lax.ppermute(value, axis, [(source, source + steps) for source in range(initial, last)])


def rms_norm(values):
    return values * lax.rsqrt(jnp.mean(values * values, axis=-1, keepdims=True) + 1e-06)


def local_core(qkv_rows):
    total = qkv_rows.shape[0]
    groups = total // PATCH
    width = qkv_rows.shape[1] // 3
    parts = qkv_rows.reshape(groups, PATCH, 3, LOCAL_HEADS, LOCAL_HEAD_DIM)
    queries = rms_norm(parts[:, :, 0])
    keys_all = rms_norm(parts[:, :, 1])
    values = parts[:, :, 2]
    scores = jnp.einsum("npha,nqha->nhpq", queries, keys_all) / math.sqrt(LOCAL_HEAD_DIM)
    causal = jnp.arange(PATCH)[:, None] >= jnp.arange(PATCH)[None, :]
    weights = jnp.where(causal[None, None], jnp.exp(scores), 0.0)
    numerator = jnp.einsum("nhpq,nqha->npha", weights, values)
    denominator = jnp.sum(weights, axis=-1).transpose(0, 2, 1)[..., None]
    return (numerator / denominator).reshape(total, width)


def local_pass(state, local_qkv, local_out, cotangent):
    layer = 0
    normed = rms_norm(state).astype(jnp.bfloat16)
    qkv_rows = jnp.dot(normed, local_qkv[layer], preferred_element_type=jnp.float32)
    core, core_back = jax.vjp(local_core, qkv_rows)
    attended = core.astype(jnp.bfloat16)
    saved = [(state, normed, core_back, attended)]
    state = state + jnp.dot(attended, local_out[layer], preferred_element_type=jnp.float32)
    hidden = state.astype(jnp.bfloat16)
    grad_state = cotangent.astype(jnp.float32)
    layer = 0
    before, normed, core_back, attended = saved[layer]
    grad_round = grad_state.astype(jnp.bfloat16)
    grads_out = [jnp.dot(attended.T, grad_round, preferred_element_type=jnp.float32)]
    grad_core = jnp.dot(grad_round, local_out[layer].T, preferred_element_type=jnp.float32)
    grad_rows = core_back(grad_core)[0].astype(jnp.bfloat16)
    grads_qkv = [jnp.dot(normed.T, grad_rows, preferred_element_type=jnp.float32)]
    return (hidden, jnp.stack(grads_qkv[::-1]), jnp.stack(grads_out[::-1]))


def per_device(byte_embeds, local_embeds, global_qkv, global_out, local_qkv, local_out, cotangent):
    byte_count = byte_embeds.shape[0]
    patch_count = byte_count // PATCH
    full_width = PATCH * byte_embeds.shape[1]
    patch_in = byte_embeds.reshape(patch_count, full_width).astype(jnp.float32)
    normed = rms_norm(patch_in).astype(jnp.bfloat16)
    projected = jnp.einsum(
        "nd,cdh->nch",
        lax.all_gather(normed, "tp", axis=0, tiled=True),
        global_qkv,
        preferred_element_type=jnp.float32,
    )
    shard_rows = projected.shape[0]
    head_width = global_qkv.shape[2]
    head_count = head_width // HEAD_DIM
    queries = rms_norm(projected[:, 0].reshape(shard_rows, head_count, HEAD_DIM)).astype(
        jnp.bfloat16
    )
    keys_mine = rms_norm(projected[:, 1].reshape(shard_rows, head_count, HEAD_DIM)).astype(
        jnp.bfloat16
    )
    values_mine = projected[:, 2].reshape(shard_rows, head_count, HEAD_DIM).astype(jnp.bfloat16)
    query_pos = lax.axis_index("ctx") * shard_rows + jnp.arange(shard_rows, dtype=jnp.int32)
    key_piece = lax.all_gather(keys_mine, "ctx", axis=0, tiled=True)
    value_piece = lax.all_gather(values_mine, "ctx", axis=0, tiled=True)
    key_count = key_piece.shape[0]
    scores = jnp.einsum(
        "rha,kha->rhk", queries, key_piece, preferred_element_type=jnp.float32
    ) / math.sqrt(HEAD_DIM)
    key_pos = jnp.arange(key_count, dtype=jnp.int32)
    allowed = key_pos[None, None, :] <= query_pos[:, None, None]
    expo = jnp.where(allowed, jnp.exp(scores), 0.0)
    numerator = jnp.einsum(
        "rhk,kha->rha", expo.astype(jnp.bfloat16), value_piece, preferred_element_type=jnp.float32
    )
    denominator = jnp.sum(expo, axis=-1)
    numerator, denominator = (numerator, denominator)
    attended = (
        (numerator / denominator[..., None]).reshape(shard_rows, head_width).astype(jnp.bfloat16)
    )
    patch_out = lax.psum_scatter(
        jnp.dot(attended, global_out, preferred_element_type=jnp.float32).astype(jnp.bfloat16),
        "tp",
        scatter_dimension=0,
        tiled=True,
    )
    earlier_row = from_behind(patch_out[-1:], ("ctx", "tp"), 1)
    patch_out = jnp.concatenate([earlier_row, patch_out[:-1]], axis=0)
    context = patch_out.reshape(byte_count, byte_embeds.shape[1])
    state = local_embeds.astype(jnp.float32) + context.astype(jnp.float32)
    hidden, grad_qkv, grad_out = local_pass(state, local_qkv, local_out, cotangent)
    grad_qkv, grad_out = (
        lax.psum_scatter(grad_qkv, ("ctx", "tp"), scatter_dimension=1, tiled=True),
        lax.psum_scatter(grad_out, ("ctx", "tp"), scatter_dimension=1, tiled=True),
    )
    return (hidden, grad_qkv, grad_out)


def solution(mesh):
    in_specs = (
        P(("ctx", "tp"), None),
        P(("ctx", "tp"), None),
        P(None, None, "tp"),
        P("tp", None),
        P(),
        P(),
        P(("ctx", "tp"), None),
    )
    out_specs = (P(("ctx", "tp"), None), P(None, ("ctx", "tp"), None), P(None, ("ctx", "tp"), None))
    return jax.shard_map(
        per_device, mesh=mesh, in_specs=in_specs, out_specs=out_specs, check_vma=False
    )
```

profile of v0, /device:TPU:0, one launch (start us, length us, event | category | flops | bytes accessed | tf_op | source)
XLA Modules:
  0.0 1156.8 jit_solution(7614287349965638369)
XLA Ops:
  7.2 1.3 reshape.139
  8.5 1.2 multiply_reduce_fusion.6
  10.8 44.9 %all-gather.4.cloned.1.call-done = bf16[384,8192]{1,0:T(8,128)(2,1)} async-done(((bf16[24,8192]{1,0:T(8,128)(2,1)}), bf16[384,8192]{1,0:T(8,128)(2,1)}) %all-gather.4.cloned.1.call-update) | async-done | bytes 6291472 | tf_op jit(solution)/shard_map/all_gather | solution.py:67
  55.8 11.2 fusion.2
  67.1 0.9 copy-done.16
  69.2 1.7 slice.71
  70.9 2.0 iota_compare_fusion
  73.9 45.5 %all-gather.8.cloned.1.call-done = bf16[3072,2,128]{2,0,1:T(8,128)(2,1)} async-done(((bf16[384,2,128]{2,0,1:T(8,128)(2,1)}), bf16[3072,2,128]{2,0,1:T(8,128)(2,1)}) %all-gather.8.cloned.1.call-update) | async-done | bytes 1572880 | tf_op jit(solution)/shard_map/all_gather | solution.py:82
  119.4 7.9 fusion
  127.3 42.8 %all-gather.6.cloned.1.call-done = bf16[3072,2,128]{0,2,1:T(8,128)(2,1)} async-done(((bf16[384,2,128]{0,2,1:T(8,128)(2,1)}), bf16[3072,2,128]{0,2,1:T(8,128)(2,1)}) %all-gather.6.cloned.1.call-update) | async-done | bytes 1572880 | tf_op jit(solution)/shard_map/all_gather | solution.py:83
  170.1 6.6 fusion.27
  176.7 4.5 convolution_convert_fusion
  182.1 1.7 fusion.38
  183.9 66.3 %reduce-scatter.4.cloned.1.call-done = bf16[24,8192]{1,0:T(8,128)(2,1)} async-done(((bf16[384,8192]{1,0:T(8,128)(2,1)}), bf16[24,8192]{1,0:T(8,128)(2,1)}) %reduce-scatter.4.cloned.1.call-update) | async-done | bytes 393232 | tf_op jit(solution)/shard_map/reduce_scatter | solution.py:99
  251.1 1.5 collective-permute-start
  252.6 8.7 copy.36
  261.3 1.0 maximum_convert_fusion
  262.2 1.3 reshape.140
  263.7 1.1 multiply_convert_fusion
  264.8 4.3 fusion.40
  271.1 1.3 multiply_reduce_fusion.2
  273.3 3.2 convolution_bitcast_fusion.1
  276.6 1.1 negate_bitcast_fusion
  277.7 2.1 fusion.16
  281.9 1.0 fusion.30
  283.2 1.2 copy.28
  284.5 3.0 convert_element_type.83
  287.5 7.7 convolution_bitcast_fusion
  295.1 1.0 copy-done.8
  296.1 2.5 fusion.18
  298.6 630.3 %reduce-scatter.8.cloned.1.call-done = f32[1,8,1024]{2,1,0:T(8,128)} async-done(((f32[1,1024,1024]{2,1,0:T(8,128)}), f32[1,8,1024]{2,1,0:T(8,128)}) %reduce-scatter.8.cloned.1.call-update) | async-done | bytes 32784 | tf_op jit(solution)/shard_map/reduce_scatter | solution.py:112
  928.9 221.0 %reduce-scatter.6.cloned.1.call-done = f32[1,8,3072]{2,1,0:T(8,128)} async-done(((f32[1,1024,3072]{2,1,0:T(8,128)}), f32[1,8,3072]{2,1,0:T(8,128)}) %reduce-scatter.6.cloned.1.call-update) | async-done | bytes 98320 | tf_op jit(solution)/shard_map/reduce_scatter | solution.py:111
  (84 shorter events, 10.6 us)
Async XLA Ops:
  7.2 174.1 %copy-start = (bf16[1,1024,1024]{2,1,0:T(8,128)(2,1)S(1)}, bf16[1,1024,1024]{2,1,0:T(8,128)(2,1)}, u32[]{:S(2)}) copy-start(bf16[1,1024,1024]{2,1,0:T(8,128)(2,1)} %param.12) | copy-start | bytes 6291460
  7.2 48.6 %all-gather.4.cloned.1.call-start = ((), (), s32[]{:S(2)}) async-start(), calls=%async_computation.3 | async-start | bytes 6684672 | tf_op jit(solution)/shard_map/all_gather | solution.py:67
  10.8 108.7 %all-gather.8.cloned.1.call-start = ((), (), s32[]{:S(2)}) async-start(), calls=%async_computation.5 | async-start | bytes 1769472 | tf_op jit(solution)/shard_map/all_gather | solution.py:82
  67.0 1.0 copy-start.16
  69.1 101.0 %all-gather.6.cloned.1.call-start = ((), (), s32[]{:S(2)}) async-start(), calls=%async_computation.4 | async-start | bytes 1769472 | tf_op jit(solution)/shard_map/all_gather | solution.py:83
  70.9 179.3 %reduce-scatter.4.cloned.1.call-start = ((), (), s32[]{:S(2)}) async-start(), calls=%async_computation.6 | async-start | bytes 6684672 | tf_op jit(solution)/shard_map/reduce_scatter | solution.py:99
  73.9 96.2 %copy-start.11 = (pred[384,3072]{0,1:T(8,128)(4,1)S(1)}, pred[384,3072]{0,1:T(8,128)(4,1)}, u32[]{:S(2)}) copy-start(pred[384,3072]{0,1:T(8,128)(4,1)} %iota_compare_fusion) | copy-start | bytes 3538948
  170.1 6.6 copy-start.3
  181.1 1.0 copy-start.9
  181.2 747.8 %reduce-scatter.8.cloned.1.call-start = ((), (), s32[]{:S(2)}) async-start(), calls=%async_computation.8 | async-start | bytes 4227072 | tf_op jit(solution)/shard_map/reduce_scatter | solution.py:112
  251.1 10.2 collective-permute-start
  252.6 8.7 copy-start.19
  261.2 2.3 copy-start.7
  269.1 1.9 copy-start.1
  269.2 1.9 copy-start.4
  269.6 0.6 copy-start.14
  269.7 0.7 copy-start.12
  271.0 1.4 copy-start.17
  271.0 1.4 copy-start.20
  271.0 2.3 copy-start.10
  272.4 0.9 copy-start.6
  276.6 873.4 %reduce-scatter.6.cloned.1.call-start = ((), (), s32[]{:S(2)}) async-start(), calls=%async_computation.7 | async-start | bytes 12681216 | tf_op jit(solution)/shard_map/reduce_scatter | solution.py:111
  276.6 3.2 copy-start.2
  279.8 1.6 copy-start.13
  279.8 1.6 copy-start.15
  279.8 1.6 copy-start.5
  279.8 1.6 copy-start.18
  279.8 1.6 copy-start.21
  295.1 1.0 copy-start.8
  295.1 1.0 copy-start.22
Sparse Core Ops, SparseCore 0:
  10.9 44.7 all-gather.3
  69.2 50.1 all-gather.7
  121.6 48.4 all-gather.5
  181.3 68.7 reduce-scatter.3
  276.7 652.2 reduce-scatter.7
  934.4 215.5 reduce-scatter.5
where the time goes:
time: 1160 us
  waiting for transfers between devices  1050 us (91%)
  matrix products  55.6 us (5%)
  local copies, waits for them, and re-layouts  23.8 us (2%)
  between operations  14.5 us (1%)
    reduce_scatter x1, waiting for transfers between devices, per_device(): lax.psum_scatter(grad_out, ('ctx', 'tp'), scatter_dimension=1, tiled=True)  630 us
    reduce_scatter x1, waiting for transfers between devices, per_device(): lax.psum_scatter(grad_qkv, ('ctx', 'tp'), scatter_dimension=1, tiled=True)  221 us
    reduce_scatter x1, waiting for transfers between devices, per_device(): lax.psum_scatter(jnp.dot(attended, global_out, preferred_element_type=jnp...  66.3 us
    all_gather x1, waiting for transfers between devices, per_device(): key_piece = lax.all_gather(keys_mine, 'ctx', axis=0, tiled=True)  45.5 us
    all_gather x1, waiting for transfers between devices, per_device(): lax.all_gather(normed, 'tp', axis=0, tiled=True)  44.9 us
    all_gather x1, waiting for transfers between devices, per_device(): value_piece = lax.all_gather(values_mine, 'ctx', axis=0, tiled=True)  42.8 us
  transfers between devices with their start and end apart: 7, of which 6 were waited for; matrix products, arithmetic and copies ran while one was open for 4% of the time, Pallas kernels for 0%

commit v1 on v0

--- a/solution.py
+++ b/solution.py
@@ -79,7 +79,9 @@
     )
     values_mine = projected[:, 2].reshape(shard_rows, head_count, HEAD_DIM).astype(jnp.bfloat16)
     query_pos = lax.axis_index("ctx") * shard_rows + jnp.arange(shard_rows, dtype=jnp.int32)
-    key_piece = lax.all_gather(keys_mine, "ctx", axis=0, tiled=True)
+    key_piece = jnp.concatenate(
+        lax.all_to_all(jnp.stack(lax.psum(1, axis_name="ctx") * [keys_mine]), "ctx", 0, 0), 0
+    )
     value_piece = lax.all_gather(values_mine, "ctx", axis=0, tiled=True)
     key_count = key_piece.shape[0]
     scores = jnp.einsum(

time: 1160 us -> 1120 us (0.966)
  waiting for transfers between devices: 1050 us -> 1000 us
    all_gather x1 -> x0, waiting for transfers between devices: 45.5 us -> none  [per_device(): key_piece = lax.all_gather(keys_mine, 'ctx', axis=0, tiled=True)]
    all_gather x1, waiting for transfers between devices: 42.8 us -> 18.3 us  [per_device(): value_piece = lax.all_gather(values_mine, 'ctx', axis=0, tiled=True)]
    all_to_all x0 -> x1, waiting for transfers between devices: none -> 22.6 us  [per_device(): lax.all_to_all(jnp.stack(lax.psum(1, axis_name='ctx') * [keys_mine]), 'ct...]
where the time goes in v1:
time: 1120 us
  waiting for transfers between devices  1000 us (89%)
  matrix products  52.7 us (5%)
  local copies, waits for them, and re-layouts  27 us (2%)
  between operations  14.2 us (1%)
    reduce_scatter x1, waiting for transfers between devices, per_device(): lax.psum_scatter(grad_out, ('ctx', 'tp'), scatter_dimension=1, tiled=True)  630 us
    reduce_scatter x1, waiting for transfers between devices, per_device(): lax.psum_scatter(grad_qkv, ('ctx', 'tp'), scatter_dimension=1, tiled=True)  221 us
    reduce_scatter x1, waiting for transfers between devices, per_device(): lax.psum_scatter(jnp.dot(attended, global_out, preferred_element_type=jnp...  66.3 us
    all_gather x1, waiting for transfers between devices, per_device(): lax.all_gather(normed, 'tp', axis=0, tiled=True)  44.9 us
    all_to_all x1, waiting for transfers between devices, per_device(): lax.all_to_all(jnp.stack(lax.psum(1, axis_name='ctx') * [keys_mine]), 'ct...  22.6 us
  transfers between devices with their start and end apart: 7, of which 6 were waited for; matrix products, arithmetic and copies ran while one was open for 4% of the time, Pallas kernels for 0%

profile of v1, /device:TPU:0, one launch (start us, length us, event | category | flops | bytes accessed | tf_op | source)
XLA Modules:
  0.0 1115.3 jit_solution(13372892510777114004)
XLA Ops:
  7.2 1.3 reshape.146
  8.5 1.2 multiply_reduce_fusion.6
  10.8 44.9 %all-gather.3.cloned.1.call-done = bf16[384,8192]{1,0:T(8,128)(2,1)} async-done(((bf16[24,8192]{1,0:T(8,128)(2,1)}), bf16[384,8192]{1,0:T(8,128)(2,1)}) %all-gather.3.cloned.1.call-update) | async-done | bytes 6291472 | tf_op jit(solution)/shard_map/all_gather | solution.py:67
  55.8 11.2 %fusion.2 = f32[384,3,256]{0,2,1:T(8,128)S(1)} fusion(bf16[3,8192,256]{2,1,0:T(8,128)(2,1)} %param.9, bf16[384,8192]{1,0:T(8,128)(2,1)} %all-gather.3.cloned.1.call-done), kind=kOutput, calls=%fused_computation.5 | convolution fusion | flops 4831838208 | bytes 20054016 | tf_op jit(solution)/shard_map/nd,cdh->nch/dot_general | solution.py:65
  68.7 1.2 fusion.60
  70.2 1.5 stack.6
  71.6 6.6 all-to-all-start
  78.3 1.9 iota_compare_fusion
  81.3 22.6 %all-to-all-done = bf16[8,384,2,128]{3,1,2,0:T(8,128)(2,1)} async-done(((bf16[8,384,2,128]{3,1,2,0:T(8,128)(2,1)}), bf16[8,384,2,128]{3,1,2,0:T(8,128)(2,1)}, u32[]{:S(2)}, u32[]{:S(2)}) %all-to-all-start) | async-done | bytes 1572896 | tf_op jit(solution)/shard_map/all_to_all | solution.py:83
  103.9 1.6 copy.31
  105.5 5.0 fusion
  110.5 18.3 %all-gather.5.cloned.1.call-done = bf16[3072,2,128]{0,2,1:T(8,128)(2,1)} async-done(((bf16[384,2,128]{0,2,1:T(8,128)(2,1)}), bf16[3072,2,128]{0,2,1:T(8,128)(2,1)}) %all-gather.5.cloned.1.call-update) | async-done | bytes 1572880 | tf_op jit(solution)/shard_map/all_gather | solution.py:85
  128.8 6.5 fusion.27
  135.4 4.5 convolution_convert_fusion
  140.9 1.7 fusion.38
  142.6 66.3 %reduce-scatter.4.cloned.1.call-done = bf16[24,8192]{1,0:T(8,128)(2,1)} async-done(((bf16[384,8192]{1,0:T(8,128)(2,1)}), bf16[24,8192]{1,0:T(8,128)(2,1)}) %reduce-scatter.4.cloned.1.call-update) | async-done | bytes 393232 | tf_op jit(solution)/shard_map/reduce_scatter | solution.py:101
  209.8 1.5 collective-permute-start
  211.3 8.7 copy.47
  221.0 1.3 reshape.147
  222.5 1.1 multiply_convert_fusion
  223.6 4.3 fusion.40
  229.8 1.3 multiply_reduce_fusion.2
  232.1 3.2 convolution_bitcast_fusion.1
  235.4 1.1 negate_bitcast_fusion
  236.4 2.1 fusion.16
  240.7 1.0 fusion.30
  241.9 1.2 copy.39
  243.2 3.0 convert_element_type.85
  246.2 7.7 convolution_bitcast_fusion
  254.8 2.5 fusion.18
  257.4 630.3 %reduce-scatter.8.cloned.1.call-done = f32[1,8,1024]{2,1,0:T(8,128)} async-done(((f32[1,1024,1024]{2,1,0:T(8,128)}), f32[1,8,1024]{2,1,0:T(8,128)}) %reduce-scatter.8.cloned.1.call-update) | async-done | bytes 32784 | tf_op jit(solution)/shard_map/reduce_scatter | solution.py:114
  887.7 221.1 %reduce-scatter.6.cloned.1.call-done = f32[1,8,3072]{2,1,0:T(8,128)} async-done(((f32[1,1024,3072]{2,1,0:T(8,128)}), f32[1,8,3072]{2,1,0:T(8,128)}) %reduce-scatter.6.cloned.1.call-update) | async-done | bytes 98320 | tf_op jit(solution)/shard_map/reduce_scatter | solution.py:113
  (87 shorter events, 13.4 us)
Async XLA Ops:
  7.2 132.8 %copy-start = (bf16[1,1024,1024]{2,1,0:T(8,128)(2,1)S(1)}, bf16[1,1024,1024]{2,1,0:T(8,128)(2,1)}, u32[]{:S(2)}) copy-start(bf16[1,1024,1024]{2,1,0:T(8,128)(2,1)} %param.12) | copy-start | bytes 6291460
  7.2 48.6 %all-gather.3.cloned.1.call-start = ((), (), s32[]{:S(2)}) async-start(), calls=%async_computation.4 | async-start | bytes 6684672 | tf_op jit(solution)/shard_map/all_gather | solution.py:67
  10.8 118.0 %all-gather.5.cloned.1.call-start = ((), (), s32[]{:S(2)}) async-start(), calls=%async_computation.5 | async-start | bytes 1769472 | tf_op jit(solution)/shard_map/all_gather | solution.py:85
  67.0 1.0 copy-start.16
  71.6 32.2 %all-to-all-start = ((bf16[8,384,2,128]{3,1,2,0:T(8,128)(2,1)}), bf16[8,384,2,128]{3,1,2,0:T(8,128)(2,1)}, u32[]{:S(2)}, u32[]{:S(2)}) async-start(bf16[8,384,2,128]{3,1,2,0:T(8,128)(2,1)} %stack.6), calls=%async_computation | async-start | bytes 3145728 | tf_op jit(solution)/shard_map/all_to_all | solution.py:83
  78.3 130.6 %reduce-scatter.4.cloned.1.call-start = ((), (), s32[]{:S(2)}) async-start(), calls=%async_computation.6 | async-start | bytes 6684672 | tf_op jit(solution)/shard_map/reduce_scatter | solution.py:101
  81.2 24.2 %copy-start.11 = (pred[384,3072]{0,1:T(8,128)(4,1)S(1)}, pred[384,3072]{0,1:T(8,128)(4,1)}, u32[]{:S(2)}) copy-start(pred[384,3072]{0,1:T(8,128)(4,1)} %iota_compare_fusion) | copy-start | bytes 3538948
  103.9 1.6 copy-start.20
  128.8 6.6 copy-start.3
  139.9 1.0 copy-start.9
  139.9 747.8 %reduce-scatter.8.cloned.1.call-start = ((), (), s32[]{:S(2)}) async-start(), calls=%async_computation.8 | async-start | bytes 4227072 | tf_op jit(solution)/shard_map/reduce_scatter | solution.py:114
  209.8 10.2 collective-permute-start
  211.3 8.7 copy-start.19
  220.0 2.3 copy-start.7
  227.9 1.9 copy-start.1
  227.9 1.9 copy-start.4
  228.4 0.6 copy-start.14
  228.4 0.7 copy-start.12
  229.7 1.4 copy-start.17
  229.7 1.4 copy-start.21
  229.7 2.3 copy-start.10
  231.1 0.9 copy-start.6
  235.3 873.4 %reduce-scatter.6.cloned.1.call-start = ((), (), s32[]{:S(2)}) async-start(), calls=%async_computation.7 | async-start | bytes 12681216 | tf_op jit(solution)/shard_map/reduce_scatter | solution.py:113
  235.3 3.2 copy-start.2
  238.5 1.6 copy-start.13
  238.5 1.6 copy-start.15
  238.6 1.6 copy-start.5
  238.6 1.6 copy-start.18
  238.6 1.6 copy-start.22
  253.8 1.0 copy-start.8
  253.8 1.0 copy-start.23
Sparse Core Ops, SparseCore 0:
  10.9 44.7 all-gather.2
  68.9 59.9 all-gather.4
  140.0 68.7 reduce-scatter.3
  235.4 652.2 reduce-scatter.7
  893.1 215.6 reduce-scatter.5
